TPU v7x, 256 devices: a whole 4x4x8 slice. The times are simulated.
256 devices in a mesh: section: 4 (over x), dp: 2 (over core), expert: 32 (over z, y).
Axes of the slice: x: 4, y: 4, z: 8, core: 2. Of those that a mesh axis runs over, the one named last changes fastest.
Arguments:
- tokens: bfloat16 [4, 8192, 2048], P('section', ('dp', 'expert')), may hold values from -6 to 6
- out_grad: bfloat16 [4, 8192, 2048], P('section', ('dp', 'expert')), may hold values from -6 to 6
- expert_ids: int32 [4, 8192, 2], P('section', ('dp', 'expert')), may hold values from 0 to 31, all different within a row; in each aligned block of 128 rows (0 to 127, 128 to 255, ..., all dimensions but the last counted through in order) at most 16 rows name the same one
- route_probs: float32 [4, 8192, 2], P('section', ('dp', 'expert')), may hold values from 0.1 to 1
- gate_weight: bfloat16 [4, 32, 2048, 768], P('section', 'expert', None, 'dp'), may hold values from -0.125 to 0.125
- up_weight: bfloat16 [4, 32, 2048, 768], P('section', 'expert', None, 'dp'), may hold values from -0.125 to 0.125
- down_weight: bfloat16 [4, 32, 768, 2048], P('section', 'expert', 'dp'), may hold values from -0.21875 to 0.21875
Outputs:
- grad_in: bfloat16 [4, 8192, 2048], P('section', ('dp', 'expert'))
- prob_grad: float32 [4, 8192, 2], P('section', ('dp', 'expert'))
- gate_weight_grad: bfloat16 [4, 32, 2048, 768], P('section', 'expert', None, 'dp')
- up_weight_grad: bfloat16 [4, 32, 2048, 768], P('section', 'expert', None, 'dp')
- down_weight_grad: bfloat16 [4, 32, 768, 2048], P('section', 'expert', 'dp')
Inputs may be any that keep to these rules, and one draw needn't show every extreme that they name: `expert_ids`: each token names 2 different experts; among the 128 tokens of one device (aligned blocks of 128 tokens of a section) no expert is named more than 16 times, a bound that some block reaches.
All inputs are finite; a program needn't handle non-finite values.
Results may differ from a plain program's by a relative error of at most 0.023.
Values may be sent and summed in bfloat16 or wider, within the bound.
A program may use at most 128 MiB of HBM per device.

v0:
```python
import jax
import jax.numpy as jnp
from jax import lax
from jax.sharding import PartitionSpec as P


def from_behind(shard, axis, by):
    length = lax.axis_size(axis)
    return lax.ppermute(shard, axis, [(i, (i + by) % length) for i in range(length)])


def expert_grads(rows_in, grads_in, weights_in, gate_part, up_part, down_part):
    contract_last = (((1,), (1,)), ((), ()))
    contract_first = (((0,), (0,)), ((), ()))
    gate_pre = jnp.dot(rows_in, gate_part, preferred_element_type=jnp.float32)
    up_pre = jnp.dot(rows_in, up_part, preferred_element_type=jnp.float32)
    sigmoid_gate = jax.nn.sigmoid(gate_pre)
    activated = gate_pre * sigmoid_gate * up_pre
    scaled_act = (weights_in[:, None] * activated).astype(jnp.bfloat16)
    hidden_grad = lax.dot_general(
        grads_in, down_part, contract_last, preferred_element_type=jnp.float32
    )
    prob_part = jnp.sum(activated * hidden_grad, axis=1)
    hidden_scaled = weights_in[:, None] * hidden_grad
    gate_grad = (
        hidden_scaled * up_pre * sigmoid_gate * (1.0 + gate_pre * (1.0 - sigmoid_gate))
    ).astype(jnp.bfloat16)
    up_grad = (hidden_scaled * gate_pre * sigmoid_gate).astype(jnp.bfloat16)
    route_dx = lax.dot_general(
        gate_grad, gate_part, contract_last, preferred_element_type=jnp.float32
    ) + lax.dot_general(up_grad, up_part, contract_last, preferred_element_type=jnp.float32)
    grad_gate = lax.dot_general(
        rows_in, gate_grad, contract_first, preferred_element_type=jnp.float32
    )
    grad_up = lax.dot_general(rows_in, up_grad, contract_first, preferred_element_type=jnp.float32)
    grad_down = lax.dot_general(
        scaled_act, grads_in, contract_first, preferred_element_type=jnp.float32
    )
    return (route_dx, prob_part, grad_gate, grad_up, grad_down)


def per_device(tokens, out_grad, expert_ids, route_probs, gate_weight, up_weight, down_weight):
    local_tokens = tokens[0]
    local_grads = out_grad[0]
    tok_count, row_width = local_tokens.shape
    top_count = expert_ids.shape[2]
    groups = lax.axis_size("expert")
    capacity = 2 * tok_count * top_count // groups
    slots_all = groups * capacity
    route_ids = expert_ids[0].reshape(-1)
    hit_table = (route_ids[:, None] == jnp.arange(groups, dtype=jnp.int32)[None, :]).astype(
        jnp.int32
    )
    before = jnp.cumsum(hit_table, axis=0) - hit_table
    slot_rank = jnp.sum(before * hit_table, axis=1)
    slot_of = route_ids * capacity + slot_rank
    placed = slot_of[None, :] == jnp.arange(slots_all, dtype=jnp.int32)[:, None]
    per_token = jnp.any(placed.reshape(slots_all, tok_count, top_count), axis=2).astype(
        jnp.bfloat16
    )
    send_rows = jnp.dot(per_token, local_tokens, preferred_element_type=jnp.float32).astype(
        jnp.bfloat16
    )
    send_grads = jnp.dot(per_token, local_grads, preferred_element_type=jnp.float32).astype(
        jnp.bfloat16
    )
    probs_flat = route_probs[0].reshape(-1)
    send_probs = jnp.sum(jnp.where(placed, probs_flat[None, :], 0.0), axis=1)
    recv_rows, recv_grads, recv_probs = (
        lax.all_to_all(
            send_rows.reshape(groups, capacity, row_width),
            "expert",
            split_axis=0,
            concat_axis=0,
            tiled=True,
        ),
        lax.all_to_all(
            send_grads.reshape(groups, capacity, row_width),
            "expert",
            split_axis=0,
            concat_axis=0,
            tiled=True,
        ),
        lax.all_to_all(
            send_probs.reshape(groups, capacity).astype(jnp.bfloat16),
            "expert",
            split_axis=0,
            concat_axis=0,
            tiled=True,
        ).astype(jnp.float32),
    )
    recv_rows = recv_rows.reshape(slots_all, row_width)
    recv_grads = recv_grads.reshape(slots_all, row_width)
    recv_probs = recv_probs.reshape(slots_all)
    gate_part = gate_weight[0, 0]
    up_part = up_weight[0, 0]
    down_part = down_weight[0, 0]
    gate_full, up_full, down_full = (
        lax.all_gather(gate_part, "dp", axis=1, tiled=True),
        lax.all_gather(up_part, "dp", axis=1, tiled=True),
        lax.all_gather(down_part, "dp", axis=0, tiled=True),
    )
    route_dx, prob_part, grad_gate, grad_up, grad_down = expert_grads(
        recv_rows, recv_grads, recv_probs, gate_full, up_full, down_full
    )
    grad_gate, grad_up, grad_down = (
        lax.psum_scatter(
            grad_gate.astype(jnp.bfloat16), "dp", scatter_dimension=1, tiled=True
        ).astype(jnp.float32),
        lax.psum_scatter(
            grad_up.astype(jnp.bfloat16), "dp", scatter_dimension=1, tiled=True
        ).astype(jnp.float32),
        lax.psum_scatter(
            grad_down.astype(jnp.bfloat16), "dp", scatter_dimension=0, tiled=True
        ).astype(jnp.float32),
    )
    back_rows, back_probs = (
        lax.all_to_all(
            route_dx.astype(jnp.bfloat16).reshape(groups, capacity, row_width),
            "expert",
            split_axis=0,
            concat_axis=0,
            tiled=True,
        ),
        lax.all_to_all(
            prob_part.reshape(groups, capacity).astype(jnp.bfloat16),
            "expert",
            split_axis=0,
            concat_axis=0,
            tiled=True,
        ).astype(jnp.float32),
    )
    token_grad = lax.dot_general(
        per_token,
        back_rows.reshape(slots_all, row_width),
        (((0,), (0,)), ((), ())),
        preferred_element_type=jnp.float32,
    ).astype(jnp.bfloat16)
    route_grad = jnp.sum(jnp.where(placed, back_probs.reshape(slots_all)[:, None], 0.0), axis=0)
    route_grad = route_grad.reshape(tok_count, top_count)
    upstream = from_behind(token_grad, "section", -1)
    return (
        upstream[None],
        route_grad[None],
        grad_gate.astype(jnp.bfloat16)[None, None],
        grad_up.astype(jnp.bfloat16)[None, None],
        grad_down.astype(jnp.bfloat16)[None, None],
    )


def solution(mesh):
    in_specs = (
        P("section", ("dp", "expert"), None),
        P("section", ("dp", "expert"), None),
        P("section", ("dp", "expert"), None),
        P("section", ("dp", "expert"), None),
        P("section", "expert", None, "dp"),
        P("section", "expert", None, "dp"),
        P("section", "expert", "dp", None),
    )
    out_specs = (
        P("section", ("dp", "expert"), None),
        P("section", ("dp", "expert"), None),
        P("section", "expert", None, "dp"),
        P("section", "expert", None, "dp"),
        P("section", "expert", "dp", None),
    )
    return jax.shard_map(
        per_device, mesh=mesh, in_specs=in_specs, out_specs=out_specs, check_vma=False
    )
```

profile of v0, /device:TPU:6, one launch (start us, length us, event | category | flops | bytes accessed | tf_op | source)
XLA Modules:
  0.0 274.5 jit_solution(8630525464374877536)
XLA Ops:
  7.2 0.7 all-gather.11.cloned.1.call-update
  7.9 0.8 copy.27
  8.7 0.1 eq.49
  8.8 0.1 eq.45
  9.0 0.6 reduce-window.6
  9.6 0.2 slice_reduce_fusion
  9.8 0.1 fusion.18
  9.9 0.1 reduce_sum.39
  10.2 2.0 convolution_convert_fusion.3
  12.3 11.6 %all-to-all-start.2 = ((bf16[32,16,2048]{2,1,0:T(8,128)(2,1)}), bf16[32,16,2048]{2,1,0:T(8,128)(2,1)S(1)}, u32[]{:S(2)}, u32[]{:S(2)}) async-start(bf16[32,16,2048]{2,1,0:T(8,128)(2,1)} %bitcast.7), calls=%async_computation.2 | async-start | bytes 4194304 | tf_op jit(solution)/shard_map/all_to_all | solution.py:70
  24.0 0.7 all-gather.9.cloned.1.call-update
  24.7 2.0 convolution_convert_fusion.4
  26.7 47.4 %all-to-all-done.2 = bf16[32,16,2048]{2,1,0:T(8,128)(2,1)S(1)} async-done(((bf16[32,16,2048]{2,1,0:T(8,128)(2,1)}), bf16[32,16,2048]{2,1,0:T(8,128)(2,1)S(1)}, u32[]{:S(2)}, u32[]{:S(2)}) %all-to-all-start.2) | async-done | bytes 2097184 | tf_op jit(solution)/shard_map/all_to_all | solution.py:70
  74.1 6.1 %all-to-all-start.1 = ((bf16[32,16,2048]{2,1,0:T(8,128)(2,1)}), bf16[32,16,2048]{2,1,0:T(8,128)(2,1)}, u32[]{:S(2)}, u32[]{:S(2)}) async-start(bf16[32,16,2048]{2,1,0:T(8,128)(2,1)} %bitcast.3), calls=%async_computation.1 | async-start | bytes 4194304 | tf_op jit(solution)/shard_map/all_to_all | solution.py:77
  80.2 0.7 all-gather.7.cloned.1.call-update
  80.9 4.8 %fusion.2 = f32[512,768]{1,0:T(8,128)} fusion(bf16[512,2048]{1,0:T(8,128)(2,1)S(1)} %bitcast.75, bf16[1,1,2048,768]{3,2,1,0:T(8,128)(2,1)} %all-gather.11.cloned.1.call-done), kind=kOutput, calls=%fused_computation.6 | convolution fusion | flops 1610612736 | bytes 6815744 | tf_op jit(solution)/shard_map/dot_general | solution.py:15
  85.7 4.8 %fusion.6 = f32[512,768]{1,0:T(8,128)} fusion(bf16[512,2048]{1,0:T(8,128)(2,1)S(1)} %bitcast.76, bf16[1,1,2048,768]{3,2,1,0:T(8,128)(2,1)} %all-gather.9.cloned.1.call-done), kind=kOutput, calls=%fused_computation.10 | convolution fusion | flops 1610612736 | bytes 6815744 | tf_op jit(solution)/shard_map/dot_general | solution.py:16
  90.6 10.8 %all-gather.7.cloned.1.call-done = bf16[1,1,768,2048]{3,2,1,0:T(8,128)(2,1)} async-done(((bf16[1,1,384,2048]{3,2,1,0:T(8,128)(2,1)}), bf16[1,1,768,2048]{3,2,1,0:T(8,128)(2,1)}) %all-gather.7.cloned.1.call-update) | async-done | bytes 3145744 | tf_op jit(solution)/shard_map/all_gather | solution.py:101
  101.4 27.9 %all-to-all-done.1 = bf16[32,16,2048]{2,1,0:T(8,128)(2,1)} async-done(((bf16[32,16,2048]{2,1,0:T(8,128)(2,1)}), bf16[32,16,2048]{2,1,0:T(8,128)(2,1)}, u32[]{:S(2)}, u32[]{:S(2)}) %all-to-all-start.1) | async-done | bytes 2097184 | tf_op jit(solution)/shard_map/all_to_all | solution.py:77
  129.3 6.5 %multiply_reduce_fusion = (bf16[512]{0:T(512)(128)(2,1)S(1)}, f32[512,768]{1,0:T(8,128)}) fusion(f32[512,768]{1,0:T(8,128)} %fusion.6, f32[512,768]{1,0:T(8,128)} %fusion.2, bf16[512,2048]{1,0:T(8,128)(2,1)} %bitcast.4, bf16[1,1,768,2048]{3,2,1,0:T(8,128)(2,1)} %all-gather.7.cloned.1.call-done), kind=kOutput, calls=%fused_computation.18 | convolution fusion | flops 1613364736 | bytes 9962496 | tf_op jit(solution)/shard_map/dot_general | solution.py:20
  135.7 0.7 convert_element_type.113
  136.4 5.9 %all-to-all-start.4 = ((bf16[32,1,16]{2,1,0:T(2,128)(2,1)}), bf16[32,1,16]{2,1,0:T(2,128)(2,1)S(1)}, u32[]{:S(2)}, u32[]{:S(2)}) async-start(bf16[32,1,16]{2,1,0:T(2,128)(2,1)} %convert_element_type.113), calls=%async_computation.4 | async-start | bytes 32768 | tf_op jit(solution)/shard_map/all_to_all | solution.py:125
  142.5 0.1 copy.32
  142.6 0.1 broadcast_in_dim.39
  142.7 9.3 %all-to-all-done.4 = bf16[32,1,16]{2,1,0:T(2,128)(2,1)S(1)} async-done(((bf16[32,1,16]{2,1,0:T(2,128)(2,1)}), bf16[32,1,16]{2,1,0:T(2,128)(2,1)S(1)}, u32[]{:S(2)}, u32[]{:S(2)}) %all-to-all-start.4) | async-done | bytes 1056 | tf_op jit(solution)/shard_map/all_to_all | solution.py:125
  152.2 0.3 select_reduce_fusion
  152.4 0.1 convert_element_type.112
  152.5 12.7 %all_to_all.27 = bf16[32,1,16]{2,1,0:T(2,128)(2,1)S(1)} all-to-all(bf16[32,1,16]{2,1,0:T(2,128)(2,1)S(1)} %convert_element_type.112), channel_id=1, replica_groups=mesh['section'=4,'dp'=2,'expert'=32] {'expert'}, dimensions={0} | all-to-all | bytes 2048 | tf_op jit(solution)/shard_map/all_to_all | solution.py:84
  165.4 3.1 %multiply_convert_fusion.1 = (bf16[512,768]{1,0:T(8,128)(2,1)S(1)}, bf16[512,768]{1,0:T(8,128)(2,1)S(1)}) fusion(f32[512,768]{1,0:T(8,128)} %fusion.2, f32[512,768]{1,0:T(8,128)} %get-tuple-element.25, f32[512]{0:T(512)S(1)} %reshape.116, f32[512,768]{1,0:T(8,128)} %fusion.6), kind=kLoop, calls=%fused_computation.20 | loop fusion | flops 5505024 | bytes 6293504 | tf_op jit(solution)/shard_map/convert_element_type | solution.py:28
  168.5 0.9 copy-done.2
  169.4 3.5 %convolution_convert_fusion.2 = bf16[2048,768]{1,0:T(8,128)(2,1)} fusion(bf16[512,2048]{1,0:T(8,128)(2,1)S(1)} %bitcast.77, bf16[512,768]{1,0:T(8,128)(2,1)S(1)} %get-tuple-element.23), kind=kOutput, calls=%fused_computation.3 | convolution fusion | flops 1612185600 | bytes 6029312 | tf_op jit(solution)/shard_map/dot_general | solution.py:32
  172.8 4.8 %copy.36 = bf16[2048,768]{0,1:T(8,128)(2,1)} copy(bf16[2048,768]{1,0:T(8,128)(2,1)} %convolution_convert_fusion.2) | data formatting | bytes 6291456
  177.7 3.5 %convolution_convert_fusion.1 = bf16[2048,768]{1,0:T(8,128)(2,1)} fusion(bf16[512,2048]{1,0:T(8,128)(2,1)S(1)} %bitcast.78, bf16[512,768]{1,0:T(8,128)(2,1)S(1)} %get-tuple-element.22), kind=kOutput, calls=%fused_computation.2 | convolution fusion | flops 1612185600 | bytes 6029312 | tf_op jit(solution)/shard_map/dot_general | solution.py:35
  181.2 4.9 %copy.38 = bf16[2048,768]{0,1:T(8,128)(2,1)} copy(bf16[2048,768]{1,0:T(8,128)(2,1)} %convolution_convert_fusion.1) | data formatting | bytes 6291456
  186.2 1.4 copy-done.1
  187.6 5.8 %convolution_convert_fusion = bf16[768,2048]{1,0:T(8,128)(2,1)} fusion(bf16[512,2048]{1,0:T(8,128)(2,1)} %bitcast.4, f32[512]{0:T(512)S(1)} %reshape.116, f32[512,768]{1,0:T(8,128)} %fusion.6, f32[512,768]{1,0:T(8,128)S(1)} %copy-done.1), kind=kOutput, calls=%fused_computation.1 | convolution fusion | flops 1614938112 | bytes 8390656 | tf_op jit(solution)/shard_map/dot_general | solution.py:36
  193.4 1.1 copy-done.3
  194.6 3.9 %fusion = f32[512,2048]{1,0:T(8,128)S(1)} fusion(bf16[512,768]{1,0:T(8,128)(2,1)S(1)} %copy-done.3, bf16[1,1,2048,768]{3,2,1,0:T(8,128)(2,1)} %all-gather.11.cloned.1.call-done), kind=kOutput, calls=%fused_computation.4 | convolution fusion | flops 1610612736 | bytes 8126464 | tf_op jit(solution)/shard_map/dot_general | solution.py:29
  198.4 1.8 add_convert_fusion
  200.3 50.4 %all_to_all.28 = bf16[32,16,2048]{2,1,0:T(8,128)(2,1)S(1)} all-to-all(bf16[32,16,2048]{2,1,0:T(8,128)(2,1)S(1)} %bitcast.79), channel_id=1, replica_groups=mesh['section'=4,'dp'=2,'expert'=32] {'expert'}, dimensions={0} | all-to-all | bytes 4194304 | tf_op jit(solution)/shard_map/all_to_all | solution.py:118
  250.7 0.5 convolution_convert_fusion.5
  251.2 0.9 collective-permute-start
  252.1 0.1 broadcast_in_dim_reshape.2
  252.3 0.6 copy.35
  252.9 8.8 %collective-permute-done = bf16[128,2048]{1,0:T(8,128)(2,1)S(1)} collective-permute-done((bf16[128,2048]{1,0:T(8,128)(2,1)S(1)}, bf16[128,2048]{1,0:T(8,128)(2,1)S(1)}, u32[]{:S(2)}, u32[]{:S(2)}) %collective-permute-start) | collective-permute-done | bytes 524320 | tf_op jit(solution)/shard_map/ppermute | solution.py:9
  261.7 2.6 copy.37
  264.3 2.6 copy.39
  266.8 0.8 copy.43
  (36 shorter events, 0.8 us)
Async XLA Ops:
  7.2 3.1 %copy-start = (bf16[1,128,2048]{2,1,0:T(8,128)(2,1)S(1)}, bf16[1,128,2048]{2,1,0:T(8,128)(2,1)}, u32[]{:S(2)}) copy-start(bf16[1,128,2048]{2,1,0:T(8,128)(2,1)} %param.7) | copy-start | bytes 1572868
  7.2 73.7 %all-gather.11.cloned.1.call-start = ((), (), s32[]{:S(2)}) async-start(), calls=%async_computation.11 | async-start | bytes 4718592 | tf_op jit(solution)/shard_map/all_gather | solution.py:99
  12.3 12.4 %copy-start.4 = (bf16[1,128,2048]{2,1,0:T(8,128)(2,1)S(1)}, bf16[1,128,2048]{2,1,0:T(8,128)(2,1)}, u32[]{:S(2)}) copy-start(bf16[1,128,2048]{2,1,0:T(8,128)(2,1)} %param.8) | copy-start | bytes 1572868
  12.3 61.8 %all-to-all-start.2 = ((bf16[32,16,2048]{2,1,0:T(8,128)(2,1)}), bf16[32,16,2048]{2,1,0:T(8,128)(2,1)S(1)}, u32[]{:S(2)}, u32[]{:S(2)}) async-start(bf16[32,16,2048]{2,1,0:T(8,128)(2,1)} %bitcast.7), calls=%async_computation.2 | async-start | bytes 4194304 | tf_op jit(solution)/shard_map/all_to_all | solution.py:70
  23.9 61.8 %all-gather.9.cloned.1.call-start = ((), (), s32[]{:S(2)}) async-start(), calls=%async_computation.10 | async-start | bytes 4718592 | tf_op jit(solution)/shard_map/all_gather | solution.py:100
  74.1 55.2 %all-to-all-start.1 = ((bf16[32,16,2048]{2,1,0:T(8,128)(2,1)}), bf16[32,16,2048]{2,1,0:T(8,128)(2,1)}, u32[]{:S(2)}, u32[]{:S(2)}) async-start(bf16[32,16,2048]{2,1,0:T(8,128)(2,1)} %bitcast.3), calls=%async_computation.1 | async-start | bytes 4194304 | tf_op jit(solution)/shard_map/all_to_all | solution.py:77
  80.1 21.3 %all-gather.7.cloned.1.call-start = ((), (), s32[]{:S(2)}) async-start(), calls=%async_computation.9 | async-start | bytes 4718592 | tf_op jit(solution)/shard_map/all_gather | solution.py:101
  129.3 13.2 %copy-start.5 = (f32[1,128,2]{1,2,0:T(2,128)S(1)}, f32[1,128,2]{1,2,0:T(2,128)}, u32[]{:S(2)}) copy-start(f32[1,128,2]{1,2,0:T(2,128)} %param.10) | copy-start | bytes 3076
  136.4 15.6 %all-to-all-start.4 = ((bf16[32,1,16]{2,1,0:T(2,128)(2,1)}), bf16[32,1,16]{2,1,0:T(2,128)(2,1)S(1)}, u32[]{:S(2)}, u32[]{:S(2)}) async-start(bf16[32,1,16]{2,1,0:T(2,128)(2,1)} %convert_element_type.113), calls=%async_computation.4 | async-start | bytes 32768 | tf_op jit(solution)/shard_map/all_to_all | solution.py:125
  142.4 119.3 %reduce-scatter.10.cloned.1.call-start = ((), (), s32[]{:S(2)}) async-start(), calls=%async_computation.12 | async-start | bytes 4718592
  168.5 0.9 copy-start.2
  177.6 86.6 %reduce-scatter.12.cloned.1.call-start = ((), (), s32[]{:S(2)}) async-start(), calls=%async_computation.13 | async-start | bytes 4718592
  186.1 1.5 copy-start.1
  186.1 80.7 %reduce-scatter.8.cloned.1.call-start = ((), (), s32[]{:S(2)}) async-start(), calls=%async_computation.8 | async-start | bytes 4718592 | tf_op jit(solution)/shard_map/reduce_scatter | solution.py:113
  193.4 1.1 copy-start.3
  194.6 3.9 %copy-start.6 = (bf16[1,1,2048,768]{3,2,1,0:T(8,128)(2,1)S(1)}, bf16[1,1,2048,768]{3,2,1,0:T(8,128)(2,1)}, u32[]{:S(2)}) copy-start(bf16[1,1,2048,768]{3,2,1,0:T(8,128)(2,1)} %all-gather.9.cloned.1.call-done) | copy-start | bytes 9437188
  251.2 10.5 %collective-permute-start = (bf16[128,2048]{1,0:T(8,128)(2,1)S(1)}, bf16[128,2048]{1,0:T(8,128)(2,1)S(1)}, u32[]{:S(2)}, u32[]{:S(2)}) collective-permute-start(bf16[128,2048]{1,0:T(8,128)(2,1)S(1)} %convolution_convert_fusion.5), channel_id=1, source_target_pairs={{0,192},{64,0},{128,64},{192,128},{1,193},{65,1},{129,65},{193,129... | collective-permute-start | bytes 1572872 | tf_op jit(solution)/shard_map/ppermute | solution.py:9
Sparse Core Ops, SparseCore 0:
  9.8 20.2 all-gather.10
  31.9 18.6 all-gather.8
  82.8 18.5 all-gather.6
  177.7 10.6 reduce-scatter.9
  190.9 17.4 reduce-scatter.11
  211.4 17.5 reduce-scatter.7
where the time goes:
time: 275 us; the launch traced here: 274 us
  waiting for transfers between devices  106 us (39%)
  blocking collectives  63.1 us (23%)
  matrix products  39.1 us (14%)
  starting transfers between devices  24.8 us (9%)
  local copies, waits for them, and re-layouts  22.5 us (8%)
  between operations  14.3 us (5%)
  other arithmetic  4.3 us (2%)
    all_to_all x1, blocking collectives, per_device(): lax.all_to_all(route_dx.astype(jnp.bfloat16).reshape(groups, capacity, ro...  50.4 us
    all_to_all x1, waiting for transfers between devices, per_device(): lax.all_to_all(send_rows.reshape(groups, capacity, row_width), 'expert',...  47.4 us
    all_to_all x1, waiting for transfers between devices, per_device(): lax.all_to_all(send_grads.reshape(groups, capacity, row_width), 'expert',...  27.9 us
    unnamed x22, local copies, waits for them, and re-layouts  20.6 us
    all_to_all x1, blocking collectives, per_device(): lax.all_to_all(send_probs.reshape(groups, capacity).astype(jnp.bfloat16),...  12.7 us
    all_to_all x1, starting transfers between devices, per_device(): lax.all_to_all(send_rows.reshape(groups, capacity, row_width), 'expert',...  11.6 us
    all_gather x1, waiting for transfers between devices, per_device(): lax.all_gather(down_part, 'dp', axis=0, tiled=True)  10.8 us
    all_to_all x1, waiting for transfers between devices, per_device(): lax.all_to_all(prob_part.reshape(groups, capacity).astype(jnp.bfloat16),...  9.33 us
  transfers between devices with their start and end apart: 10, of which 5 were waited for; matrix products, arithmetic and copies ran while one was open for 16% of the time, Pallas kernels for 0%

commit v1 on v0

--- a/solution.py
+++ b/solution.py
@@ -95,10 +95,19 @@
     gate_part = gate_weight[0, 0]
     up_part = up_weight[0, 0]
     down_part = down_weight[0, 0]
+
+    def strings_track(u, d0):
+        return jnp.concatenate(
+            lax.all_to_all(
+                jnp.stack([u for _ in range(lax.psum(1, "dp"))]), "dp", split_axis=0, concat_axis=0
+            ),
+            axis=d0,
+        )
+
     gate_full, up_full, down_full = (
         lax.all_gather(gate_part, "dp", axis=1, tiled=True),
         lax.all_gather(up_part, "dp", axis=1, tiled=True),
-        lax.all_gather(down_part, "dp", axis=0, tiled=True),
+        strings_track(down_part, 0),
     )
     route_dx, prob_part, grad_gate, grad_up, grad_down = expert_grads(
         recv_rows, recv_grads, recv_probs, gate_full, up_full, down_full

time: 275 us -> 285 us (1.036)
  starting transfers between devices: 24.8 us -> 30.1 us
  other arithmetic: 4.3 us -> 9.11 us
    all_gather x1, waiting for transfers between devices: 0.01 us -> 15.6 us  [per_device(): lax.all_gather(up_part, 'dp', axis=1, tiled=True)]
    all_gather x1 -> x0, waiting for transfers between devices: 10.8 us -> none  [per_device(): lax.all_gather(down_part, 'dp', axis=0, tiled=True)]
    all_to_all x0 -> x1, starting transfers between devices: none -> 5.32 us  [strings_track(): lax.all_to_all(jnp.stack([u for _ in range(lax.psum(1, 'dp'))]), 'dp', sp...]
    all_to_all x1, waiting for transfers between devices: 27.9 us -> 23.8 us  [per_device(): lax.all_to_all(send_grads.reshape(groups, capacity, row_width), 'expert',...]
    another operation x2 -> x3, other arithmetic: 0.63 us -> 4.56 us  [the longest x1 3.93 us: strings_track(): jnp.stack([u for _ in range(lax.psum(1, 'dp'))])]
    unnamed x22 -> x24, local copies, waits for them, and re-layouts: 20.6 us -> 19 us
  transfers between devices with their start and end apart: 10 -> 10, of which waited for: 5 -> 5; matrix products, arithmetic and copies ran while one was open for 16% -> 15% of each run, Pallas kernels for 0% -> 0%
where the time goes in v1:
time: 285 us; the launch traced here: 284 us
  waiting for transfers between devices  107 us (38%)
  blocking collectives  63.1 us (22%)
  matrix products  40.2 us (14%)
  starting transfers between devices  30.1 us (11%)
  local copies, waits for them, and re-layouts  20.9 us (7%)
  between operations  14 us (5%)
  other arithmetic  9.11 us (3%)
    all_to_all x1, blocking collectives, per_device(): lax.all_to_all(route_dx.astype(jnp.bfloat16).reshape(groups, capacity, ro...  50.4 us
    all_to_all x1, waiting for transfers between devices, per_device(): lax.all_to_all(send_rows.reshape(groups, capacity, row_width), 'expert',...  48 us
    all_to_all x1, waiting for transfers between devices, per_device(): lax.all_to_all(send_grads.reshape(groups, capacity, row_width), 'expert',...  23.8 us
    unnamed x24, local copies, waits for them, and re-layouts  19 us
    all_gather x1, waiting for transfers between devices, per_device(): lax.all_gather(up_part, 'dp', axis=1, tiled=True)  15.6 us
    all_to_all x1, blocking collectives, per_device(): lax.all_to_all(send_probs.reshape(groups, capacity).astype(jnp.bfloat16),...  12.7 us
    all_to_all x1, starting transfers between devices, per_device(): lax.all_to_all(send_rows.reshape(groups, capacity, row_width), 'expert',...  11.6 us
    all_to_all x1, waiting for transfers between devices, per_device(): lax.all_to_all(prob_part.reshape(groups, capacity).astype(jnp.bfloat16),...  9.33 us
  transfers between devices with their start and end apart: 10, of which 5 were waited for; matrix products, arithmetic and copies ran while one was open for 15% of the time, Pallas kernels for 0%

profile of v1, /device:TPU:6, one launch (start us, length us, event | category | flops | bytes accessed | tf_op | source)
XLA Modules:
  0.0 284.3 jit_solution(2692629110328732722)
XLA Ops:
  7.2 3.9 %pad_maximum_fusion = bf16[2,384,2048]{2,1,0:T(8,128)(2,1)} fusion(bf16[1,384,2048]{2,1,0:T(8,128)(2,1)} %bitcast.82), kind=kLoop, calls=%fused_computation.4 | loop fusion | flops 1572864 | bytes 4718592 | tf_op jit(solution)/shard_map/stack | solution.py:102
  11.1 5.3 %all-to-all-start.2 = ((bf16[2,384,2048]{2,1,0:T(8,128)(2,1)}), bf16[2,384,2048]{2,1,0:T(8,128)(2,1)}, u32[]{:S(2)}, u32[]{:S(2)}) async-start(bf16[2,384,2048]{2,1,0:T(8,128)(2,1)} %pad_maximum_fusion), calls=%async_computation.2 | async-start | bytes 6291456 | tf_op jit(solution)/shard_map/all_to_all | solution.py:101
  16.5 0.1 copy.27
  16.6 0.1 eq.45
  16.7 0.1 eq.49
  16.9 0.6 reduce-window.6
  17.5 0.2 slice_reduce_fusion
  17.7 0.1 fusion.16
  17.8 0.1 reduce_sum.39
  18.1 2.1 convolution_convert_fusion.3
  20.2 11.6 %all-to-all-start.3 = ((bf16[32,16,2048]{2,1,0:T(8,128)(2,1)}), bf16[32,16,2048]{2,1,0:T(8,128)(2,1)S(1)}, u32[]{:S(2)}, u32[]{:S(2)}) async-start(bf16[32,16,2048]{2,1,0:T(8,128)(2,1)} %bitcast.8), calls=%async_computation.3 | async-start | bytes 4194304 | tf_op jit(solution)/shard_map/all_to_all | solution.py:70
  31.9 0.7 all-gather.7.cloned.1.call-update
  32.6 2.0 convolution_convert_fusion.4
  34.6 48.0 %all-to-all-done.3 = bf16[32,16,2048]{2,1,0:T(8,128)(2,1)S(1)} async-done(((bf16[32,16,2048]{2,1,0:T(8,128)(2,1)}), bf16[32,16,2048]{2,1,0:T(8,128)(2,1)S(1)}, u32[]{:S(2)}, u32[]{:S(2)}) %all-to-all-start.3) | async-done | bytes 2097184 | tf_op jit(solution)/shard_map/all_to_all | solution.py:70
  82.6 6.1 %all-to-all-start.1 = ((bf16[32,16,2048]{2,1,0:T(8,128)(2,1)}), bf16[32,16,2048]{2,1,0:T(8,128)(2,1)}, u32[]{:S(2)}, u32[]{:S(2)}) async-start(bf16[32,16,2048]{2,1,0:T(8,128)(2,1)} %bitcast.3), calls=%async_computation.1 | async-start | bytes 4194304 | tf_op jit(solution)/shard_map/all_to_all | solution.py:77
  88.8 0.7 all-gather.5.cloned.1.call-update
  89.5 4.8 %fusion.2 = f32[512,768]{1,0:T(8,128)} fusion(bf16[512,2048]{1,0:T(8,128)(2,1)S(1)} %bitcast.73, bf16[1,1,2048,768]{3,2,1,0:T(8,128)(2,1)} %all-gather.7.cloned.1.call-done), kind=kOutput, calls=%fused_computation.7 | convolution fusion | flops 1610612736 | bytes 6815744 | tf_op jit(solution)/shard_map/dot_general | solution.py:15
  94.3 15.6 %all-gather.5.cloned.1.call-done = bf16[1,1,2048,768]{3,2,1,0:T(8,128)(2,1)} async-done(((bf16[1,1,2048,384]{3,2,1,0:T(8,128)(2,1)}), bf16[1,1,2048,768]{3,2,1,0:T(8,128)(2,1)}) %all-gather.5.cloned.1.call-update) | async-done | bytes 3145744 | tf_op jit(solution)/shard_map/all_gather | solution.py:109
  109.9 4.8 %fusion.6 = f32[512,768]{1,0:T(8,128)} fusion(bf16[512,2048]{1,0:T(8,128)(2,1)S(1)} %bitcast.74, bf16[1,1,2048,768]{3,2,1,0:T(8,128)(2,1)} %all-gather.5.cloned.1.call-done), kind=kOutput, calls=%fused_computation.11 | convolution fusion | flops 1610612736 | bytes 6815744 | tf_op jit(solution)/shard_map/dot_general | solution.py:16
  114.7 23.8 %all-to-all-done.1 = bf16[32,16,2048]{2,1,0:T(8,128)(2,1)} async-done(((bf16[32,16,2048]{2,1,0:T(8,128)(2,1)}), bf16[32,16,2048]{2,1,0:T(8,128)(2,1)}, u32[]{:S(2)}, u32[]{:S(2)}) %all-to-all-start.1) | async-done | bytes 2097184 | tf_op jit(solution)/shard_map/all_to_all | solution.py:77
  138.5 6.5 %multiply_reduce_fusion = (bf16[512]{0:T(512)(128)(2,1)S(1)}, f32[512,768]{1,0:T(8,128)}) fusion(f32[512,768]{1,0:T(8,128)} %fusion.6, f32[512,768]{1,0:T(8,128)} %fusion.2, bf16[512,2048]{1,0:T(8,128)(2,1)} %bitcast.4, bf16[768,2048]{1,0:T(8,128)(2,1)} %bitcast.6), kind=kOutput, calls=%fused_computation.17 | convolution fusion | flops 1613364736 | bytes 9962496 | tf_op jit(solution)/shard_map/dot_general | solution.py:20
  145.0 0.7 convert_element_type.113
  145.7 5.9 %all-to-all-start.5 = ((bf16[32,1,16]{2,1,0:T(2,128)(2,1)}), bf16[32,1,16]{2,1,0:T(2,128)(2,1)S(1)}, u32[]{:S(2)}, u32[]{:S(2)}) async-start(bf16[32,1,16]{2,1,0:T(2,128)(2,1)} %convert_element_type.113), calls=%async_computation.5 | async-start | bytes 32768 | tf_op jit(solution)/shard_map/all_to_all | solution.py:134
  151.7 0.1 copy.32
  151.8 0.1 broadcast_in_dim.39
  151.9 9.3 %all-to-all-done.5 = bf16[32,1,16]{2,1,0:T(2,128)(2,1)S(1)} async-done(((bf16[32,1,16]{2,1,0:T(2,128)(2,1)}), bf16[32,1,16]{2,1,0:T(2,128)(2,1)S(1)}, u32[]{:S(2)}, u32[]{:S(2)}) %all-to-all-start.5) | async-done | bytes 1056 | tf_op jit(solution)/shard_map/all_to_all | solution.py:134
  161.4 0.3 select_reduce_fusion
  161.7 0.1 convert_element_type.112
  161.7 12.7 %all_to_all.32 = bf16[32,1,16]{2,1,0:T(2,128)(2,1)S(1)} all-to-all(bf16[32,1,16]{2,1,0:T(2,128)(2,1)S(1)} %convert_element_type.112), channel_id=1, replica_groups=mesh['section'=4,'dp'=2,'expert'=32] {'expert'}, dimensions={0} | all-to-all | bytes 2048 | tf_op jit(solution)/shard_map/all_to_all | solution.py:84
  174.6 4.0 %multiply_convert_fusion.1 = (bf16[512,768]{1,0:T(8,128)(2,1)S(1)}, bf16[512,768]{1,0:T(8,128)(2,1)}) fusion(f32[512,768]{1,0:T(8,128)} %fusion.2, f32[512,768]{1,0:T(8,128)} %get-tuple-element.25, f32[512]{0:T(512)S(1)} %reshape.120, f32[512,768]{1,0:T(8,128)} %fusion.6), kind=kLoop, calls=%fused_computation.19 | loop fusion | flops 5505024 | bytes 6293504 | tf_op jit(solution)/shard_map/convert_element_type | solution.py:28
  178.6 3.5 %convolution_convert_fusion.1 = bf16[2048,768]{1,0:T(8,128)(2,1)} fusion(bf16[512,2048]{1,0:T(8,128)(2,1)S(1)} %bitcast.75, bf16[512,768]{1,0:T(8,128)(2,1)S(1)} %get-tuple-element.22), kind=kOutput, calls=%fused_computation.2 | convolution fusion | flops 1612185600 | bytes 6029312 | tf_op jit(solution)/shard_map/dot_general | solution.py:35
  182.0 4.8 %copy.38 = bf16[2048,768]{0,1:T(8,128)(2,1)} copy(bf16[2048,768]{1,0:T(8,128)(2,1)} %convolution_convert_fusion.1) | data formatting | bytes 6291456
  186.9 4.6 %convolution_convert_fusion.2 = bf16[2048,768]{1,0:T(8,128)(2,1)} fusion(bf16[512,2048]{1,0:T(8,128)(2,1)S(1)} %bitcast.76, bf16[512,768]{1,0:T(8,128)(2,1)} %get-tuple-element.23), kind=kOutput, calls=%fused_computation.3 | convolution fusion | flops 1612185600 | bytes 6029312 | tf_op jit(solution)/shard_map/dot_general | solution.py:32
  191.5 4.8 %copy.36 = bf16[2048,768]{0,1:T(8,128)(2,1)} copy(bf16[2048,768]{1,0:T(8,128)(2,1)} %convolution_convert_fusion.2) | data formatting | bytes 6291456
  196.4 1.5 copy-done.2
  197.8 5.7 %convolution_convert_fusion = bf16[768,2048]{1,0:T(8,128)(2,1)} fusion(bf16[512,2048]{1,0:T(8,128)(2,1)} %bitcast.4, f32[512]{0:T(512)S(1)} %reshape.120, f32[512,768]{1,0:T(8,128)} %fusion.6, f32[512,768]{1,0:T(8,128)S(1)} %copy-done.2), kind=kOutput, calls=%fused_computation.1 | convolution fusion | flops 1614938112 | bytes 8390656 | tf_op jit(solution)/shard_map/dot_general | solution.py:36
  203.6 1.1 copy-done.3
  204.7 3.9 %fusion = f32[512,2048]{1,0:T(8,128)S(1)} fusion(bf16[512,768]{1,0:T(8,128)(2,1)S(1)} %copy-done.3, bf16[1,1,2048,768]{3,2,1,0:T(8,128)(2,1)} %all-gather.7.cloned.1.call-done), kind=kOutput, calls=%fused_computation.5 | convolution fusion | flops 1610612736 | bytes 8126464 | tf_op jit(solution)/shard_map/dot_general | solution.py:29
  208.5 1.8 add_convert_fusion
  210.4 50.4 %all_to_all.33 = bf16[32,16,2048]{2,1,0:T(8,128)(2,1)S(1)} all-to-all(bf16[32,16,2048]{2,1,0:T(8,128)(2,1)S(1)} %bitcast.77), channel_id=1, replica_groups=mesh['section'=4,'dp'=2,'expert'=32] {'expert'}, dimensions={0} | all-to-all | bytes 4194304 | tf_op jit(solution)/shard_map/all_to_all | solution.py:127
  260.8 0.5 convolution_convert_fusion.5
  261.3 0.9 collective-permute-start
  262.2 0.1 broadcast_in_dim_reshape.2
  262.3 0.6 copy.35
  263.0 8.8 %collective-permute-done = bf16[128,2048]{1,0:T(8,128)(2,1)S(1)} collective-permute-done((bf16[128,2048]{1,0:T(8,128)(2,1)S(1)}, bf16[128,2048]{1,0:T(8,128)(2,1)S(1)}, u32[]{:S(2)}, u32[]{:S(2)}) %collective-permute-start) | collective-permute-done | bytes 524320 | tf_op jit(solution)/shard_map/ppermute | solution.py:9
  271.8 2.6 copy.39
  274.3 2.6 copy.37
  277.0 0.8 copy.43
  (38 shorter events, 0.8 us)
Async XLA Ops:
  7.2 10.9 %copy-start = (bf16[1,128,2048]{2,1,0:T(8,128)(2,1)S(1)}, bf16[1,128,2048]{2,1,0:T(8,128)(2,1)}, u32[]{:S(2)}) copy-start(bf16[1,128,2048]{2,1,0:T(8,128)(2,1)} %param.7) | copy-start | bytes 1572868
  11.1 5.3 %copy-start.5 = (s32[1,128,2]{1,2,0:T(2,128)S(1)}, s32[1,128,2]{1,2,0:T(2,128)}, u32[]{:S(2)}) copy-start(s32[1,128,2]{1,2,0:T(2,128)} %param.9) | copy-start | bytes 3076
  11.1 9.1 %all-to-all-start.2 = ((bf16[2,384,2048]{2,1,0:T(8,128)(2,1)}), bf16[2,384,2048]{2,1,0:T(8,128)(2,1)}, u32[]{:S(2)}, u32[]{:S(2)}) async-start(bf16[2,384,2048]{2,1,0:T(8,128)(2,1)} %pad_maximum_fusion), calls=%async_computation.2 | async-start | bytes 6291456 | tf_op jit(solution)/shard_map/all_to_all | solution.py:101
  20.2 12.4 %copy-start.4 = (bf16[1,128,2048]{2,1,0:T(8,128)(2,1)S(1)}, bf16[1,128,2048]{2,1,0:T(8,128)(2,1)}, u32[]{:S(2)}) copy-start(bf16[1,128,2048]{2,1,0:T(8,128)(2,1)} %param.8) | copy-start | bytes 1572868
  20.2 62.4 %all-to-all-start.3 = ((bf16[32,16,2048]{2,1,0:T(8,128)(2,1)}), bf16[32,16,2048]{2,1,0:T(8,128)(2,1)S(1)}, u32[]{:S(2)}, u32[]{:S(2)}) async-start(bf16[32,16,2048]{2,1,0:T(8,128)(2,1)} %bitcast.8), calls=%async_computation.3 | async-start | bytes 4194304 | tf_op jit(solution)/shard_map/all_to_all | solution.py:70
  31.8 57.7 %all-gather.7.cloned.1.call-start = ((), (), s32[]{:S(2)}) async-start(), calls=%async_computation.11 | async-start | bytes 4718592 | tf_op jit(solution)/shard_map/all_gather | solution.py:108
  82.6 55.9 %all-to-all-start.1 = ((bf16[32,16,2048]{2,1,0:T(8,128)(2,1)}), bf16[32,16,2048]{2,1,0:T(8,128)(2,1)}, u32[]{:S(2)}, u32[]{:S(2)}) async-start(bf16[32,16,2048]{2,1,0:T(8,128)(2,1)} %bitcast.3), calls=%async_computation.1 | async-start | bytes 4194304 | tf_op jit(solution)/shard_map/all_to_all | solution.py:77
  88.7 21.2 %all-gather.5.cloned.1.call-start = ((), (), s32[]{:S(2)}) async-start(), calls=%async_computation.10 | async-start | bytes 4718592 | tf_op jit(solution)/shard_map/all_gather | solution.py:109
  138.5 13.2 %copy-start.6 = (f32[1,128,2]{1,2,0:T(2,128)S(1)}, f32[1,128,2]{1,2,0:T(2,128)}, u32[]{:S(2)}) copy-start(f32[1,128,2]{1,2,0:T(2,128)} %param.10) | copy-start | bytes 3076
  145.7 15.6 %all-to-all-start.5 = ((bf16[32,1,16]{2,1,0:T(2,128)(2,1)}), bf16[32,1,16]{2,1,0:T(2,128)(2,1)S(1)}, u32[]{:S(2)}, u32[]{:S(2)}) async-start(bf16[32,1,16]{2,1,0:T(2,128)(2,1)} %convert_element_type.113), calls=%async_computation.5 | async-start | bytes 32768 | tf_op jit(solution)/shard_map/all_to_all | solution.py:134
  151.6 120.2 %reduce-scatter.12.cloned.1.call-start = ((), (), s32[]{:S(2)}) async-start(), calls=%async_computation.13 | async-start | bytes 4718592
  186.8 87.5 %reduce-scatter.10.cloned.1.call-start = ((), (), s32[]{:S(2)}) async-start(), calls=%async_computation.12 | async-start | bytes 4718592
  196.3 1.5 copy-start.2
  196.3 80.7 %reduce-scatter.8.cloned.1.call-start = ((), (), s32[]{:S(2)}) async-start(), calls=%async_computation.9 | async-start | bytes 4718592 | tf_op jit(solution)/shard_map/reduce_scatter | solution.py:122
  203.5 1.1 copy-start.3
  204.7 3.9 %copy-start.7 = (bf16[1,1,2048,768]{3,2,1,0:T(8,128)(2,1)S(1)}, bf16[1,1,2048,768]{3,2,1,0:T(8,128)(2,1)}, u32[]{:S(2)}) copy-start(bf16[1,1,2048,768]{3,2,1,0:T(8,128)(2,1)} %all-gather.5.cloned.1.call-done) | copy-start | bytes 9437188
  261.3 10.5 %collective-permute-start = (bf16[128,2048]{1,0:T(8,128)(2,1)S(1)}, bf16[128,2048]{1,0:T(8,128)(2,1)S(1)}, u32[]{:S(2)}, u32[]{:S(2)}) collective-permute-start(bf16[128,2048]{1,0:T(8,128)(2,1)S(1)} %convolution_convert_fusion.5), channel_id=1, source_target_pairs={{0,192},{64,0},{128,64},{192,128},{1,193},{65,1},{129,65},{193,129... | collective-permute-start | bytes 1572872 | tf_op jit(solution)/shard_map/ppermute | solution.py:9
  274.3 3.4 %copy-start.1 = (bf16[1,128,2048]{2,1,0:T(8,128)(2,1)S(1)}, bf16[1,128,2048]{2,1,0:T(8,128)(2,1)}, u32[]{:S(2)}) copy-start(bf16[1,128,2048]{2,1,0:T(8,128)(2,1)} %param.7) | copy-start | bytes 1572868
Sparse Core Ops, SparseCore 0:
  34.5 18.5 all-gather.6
  91.3 18.4 all-gather.4
  187.0 10.5 reduce-scatter.11
  200.1 17.5 reduce-scatter.9
  220.6 17.4 reduce-scatter.7
